TPU v7x, 128 devices: a whole 4x4x4 slice. The times are simulated.
128 devices in a mesh: grp: 8 (over z, core), col: 16 (over x, y).
Axes of the slice: x: 4, y: 4, z: 4, core: 2. Of those that a mesh axis runs over, the one named last changes fastest.
Arguments:
- pivot_blocks: float32 [8, 1024, 1024], P('grp'), as said below
- coupling: float32 [8, 4096, 1024], P('grp', 'col'), as said below
- block_map: int32 [8, 32], replicated, may hold values from 0 to 63, as said below
- parent_matrix: float32 [8192, 8192], P('grp', 'col'), as said below
Outputs:
- child_factor: float32 [8, 4096, 1024], P('grp', 'col')
- parent_factor: float32 [8192, 8192], P('grp', 'col')
Inputs may be any that keep to these rules, and one draw needn't show every extreme that they name: `block_map`: each row is strictly increasing. For every child and every aligned run of 8 parent blocks (starting at a multiple of 8), at most 6 of the row's entries fall in the run; one such run holds exactly 6 entries of every row. `pivot_blocks`: every child's block is symmetric positive definite. `coupling`: independent entries. `parent_matrix`: Symmetric, with a positive diagonal; the leading 2 * 512 rows and columns of assembled form a positive definite block.
All inputs are finite; a program needn't handle non-finite values.
Results may differ from a plain program's by a relative error of at most 0.0001.
Values sent between devices are 32-bit elements; how exact they have to be, the bound alone decides.
No kernel may reach another device: no remote copies, remote signals or barrier semaphores. Data moves between devices by JAX's collectives and lax.ppermute only.
A program may use at most 128 MiB of HBM per device.

v0:
```python
import functools

import jax
import jax.numpy as jnp
from jax import lax
from jax.experimental import pallas as pl
from jax.experimental.pallas import tpu as pltpu
from jax.sharding import PartitionSpec as P


BLK = 128
PANEL = 512
LEAD = 1024
PIV = 1024
SBLK = 32
PBLK = 64

HIGHEST = lax.Precision.HIGHEST


def eliminate(work):
    order = BLK
    lane = lax.broadcasted_iota(jnp.int32, (8, order), 1)
    sub = lax.broadcasted_iota(jnp.int32, (8, order), 0)
    parts = order // 8
    rows = [work[8 * q : 8 * q + 8, :] for q in range(parts)]
    low = [jnp.zeros((8, order), jnp.float32) for _ in range(parts)]
    for q in range(parts):
        cols = [
            [
                jnp.broadcast_to(rows[p][:, 8 * q + k : 8 * q + k + 1], (8, order))
                for p in range(q, parts)
            ]
            for k in range(8)
        ]
        here = (lane >= 8 * q) & (lane < 8 * q + 8)
        mine = jnp.where(here, jnp.where(lane == sub + 8 * q, 1.0, 0.0), rows[q])
        fresh = []
        for k in range(8):
            raw = cols[k]
            root = lax.rsqrt(jnp.broadcast_to(raw[0][k : k + 1, :], (8, order)))
            scales = [jnp.broadcast_to(raw[0][m : m + 1, :], (8, order)) for m in range(k + 1, 8)]
            row = jnp.broadcast_to(mine[k : k + 1, :], (8, order)) * root
            fresh.append(row)
            done = [c * root for c in raw]
            for m in range(k + 1, 8):
                scale = scales[m - k - 1] * root
                cols[m] = [a - b * scale for a, b in zip(cols[m], done)]
            mine = jnp.where(sub > k, mine - done[0] * row, jnp.where(sub == k, row, mine))
            cols[k] = [jnp.where(sub >= k, done[0], 0.0)] + done[1:]
        rows[q] = mine
        for p in range(q, parts):
            for k in range(8):
                low[p] = jnp.where(lane == 8 * q + k, cols[k][p - q], low[p])
        for p in range(q + 1, parts):
            acc = jnp.where(here, 0.0, rows[p])
            for k in range(8):
                acc = acc - cols[k][p - q] * fresh[k]
            rows[p] = acc
    for q in range(parts):
        rows[q] = jnp.where(lane <= sub + 8 * q, rows[q], 0.0)
    return jnp.concatenate(rows, axis=0), jnp.concatenate(low, axis=0)


def exact(a, b):
    return jnp.dot(a, b, precision=HIGHEST, preferred_element_type=jnp.float32)


def factor_steps(first, last, t_ref, l_ref, r_ref, terms=None):
    order = t_ref.shape[0]
    blocks = order // BLK

    def keep(rows):
        if terms is not None:
            terms[0][rows, :], terms[1][rows, :] = split(r_ref[rows, :])

    def change(left, rows):
        if terms is None:
            return exact(left, r_ref[rows, :])
        return product(split(left), (terms[0][rows, :], terms[1][rows, :]))

    def pair(p, carry):
        base = pl.multiple_of(p * 2 * BLK, 2 * BLK)
        out = pl.multiple_of(base - first * BLK, 2 * BLK)
        if l_ref is not None:
            l_ref[:, pl.ds(out, 2 * BLK)] = jnp.zeros((order, 2 * BLK), jnp.float32)

        def one(j, carry):
            at = pl.multiple_of(base + j * BLK, BLK)
            rows = pl.ds(pl.multiple_of(j * BLK, BLK), BLK)
            inv, low = eliminate(t_ref[pl.ds(at, BLK), pl.ds(at, BLK)])
            r_ref[rows, :] = exact(inv, t_ref[pl.ds(at, BLK), :])
            r_ref[rows, pl.ds(at, BLK)] = inv
            t_ref[pl.ds(at, BLK), :] = r_ref[rows, :]
            if l_ref is not None:
                to = pl.multiple_of(out + j * BLK, BLK)
                l_ref[pl.ds(at, BLK), pl.ds(to, BLK)] = low
            keep(rows)

            @pl.when(j == 0)
            def _():
                to = pl.multiple_of(base + BLK, BLK)
                top = slice(0, BLK)
                left = r_ref[top, pl.ds(to, BLK)].T
                if l_ref is not None:
                    l_ref[pl.ds(to, BLK), pl.ds(out, BLK)] = left
                t_ref[pl.ds(to, BLK), pl.ds(base, BLK)] = jnp.zeros((BLK, BLK), jnp.float32)
                t_ref[pl.ds(to, BLK), :] = t_ref[pl.ds(to, BLK), :] - change(left, top)
                r_ref[top, pl.ds(to, BLK)] = jnp.zeros((BLK, BLK), jnp.float32)
                keep(top)

            return carry

        lax.fori_loop(0, 2, one, 0)

        def below(i, carry):
            to = pl.multiple_of(i * BLK, BLK)
            left = r_ref[:, pl.ds(to, BLK)].T
            if l_ref is not None:
                l_ref[pl.ds(to, BLK), pl.ds(out, 2 * BLK)] = left
            t_ref[pl.ds(to, BLK), pl.ds(base, 2 * BLK)] = jnp.zeros((BLK, 2 * BLK), jnp.float32)
            t_ref[pl.ds(to, BLK), :] = t_ref[pl.ds(to, BLK), :] - change(left, slice(0, 2 * BLK))
            return carry

        return lax.fori_loop(2 * p + 2, blocks, below, carry)

    lax.fori_loop(first // 2, last // 2, pair, 0)
    if last == blocks:
        for b in range(blocks - 1):
            width = order - BLK * (b + 1)
            t_ref[BLK * b : BLK * b + BLK, BLK * (b + 1) :] = jnp.zeros((BLK, width), jnp.float32)


def child_kernel(a_ref, t_ref, r_ref):
    t_ref[...] = a_ref[...]
    factor_steps(0, PIV // BLK, t_ref, None, r_ref)


def lead_start_kernel(last, place_ref, *refs):
    pieces, (t_ref, l_ref, r_ref, *terms) = refs[:8], refs[8:]
    core, px, py = place_ref[3], place_ref[4], place_ref[5]
    half = PANEL // 2
    for sx in range(4):
        for sy in range(4):
            x, y = (px + 4 - sx) % 4, (py + 4 - sy) % 4
            where = x * 4 + y
            row = (where % 2) * PANEL
            column = pl.multiple_of((where // 2) * BLK, BLK)
            first = pl.multiple_of(row + core * half, half)
            second = pl.multiple_of(row + (1 - core) * half, half)
            t_ref[pl.ds(first, half), pl.ds(column, BLK)] = pieces[sx][sy]
            t_ref[pl.ds(second, half), pl.ds(column, BLK)] = pieces[4 + sy][sx]
    factor_steps(0, last, t_ref, l_ref, r_ref, terms)


def lead_next_kernel(first, last, t_in, t_ref, l_ref, r_ref, *terms):
    t_ref[...] = t_in[...]
    factor_steps(first, last, t_ref, l_ref, r_ref, terms)


WHOLE = pl.BlockSpec(memory_space=pltpu.VMEM)
TABLE = pl.BlockSpec(memory_space=pltpu.SMEM)


def square(order):
    return jax.ShapeDtypeStruct((order, order), jnp.float32)


def limit(mib):
    return pltpu.CompilerParams(vmem_limit_bytes=mib << 20)


def work(gflop, mib):
    return pl.CostEstimate(
        flops=int(gflop * 10**9), bytes_accessed=mib << 20, transcendentals=0
    )


def child_factor(matrix):
    return pl.pallas_call(
        child_kernel,
        out_shape=square(PIV),
        in_specs=[WHOLE],
        out_specs=WHOLE,
        scratch_shapes=[pltpu.VMEM((2 * BLK, PIV), jnp.float32)],
        cost_estimate=work(40, 12),
        compiler_params=limit(24),
        name="child_factor",
    )(matrix)


def lead_call(kernel, columns, in_specs):
    return pl.pallas_call(
        kernel,
        out_shape=[square(LEAD), jax.ShapeDtypeStruct((LEAD, columns), jnp.float32)],
        in_specs=in_specs,
        out_specs=[WHOLE] * 2,
        scratch_shapes=[pltpu.VMEM((2 * BLK, LEAD), jnp.float32)]
        + [pltpu.VMEM((2 * BLK, LEAD), jnp.bfloat16)] * 2,
        cost_estimate=work(10, 12),
        compiler_params=limit(24),
    )


def lead_start(place, pieces, last):
    kernel = functools.partial(lead_start_kernel, last)
    return lead_call(kernel, last * BLK, [TABLE] + [WHOLE] * 8)(place, *pieces)


def lead_next(t, first, last):
    kernel = functools.partial(lead_next_kernel, first, last)
    return lead_call(kernel, (last - first) * BLK, [WHOLE])(t)


def split(x):
    high = x.astype(jnp.bfloat16)
    return high, (x - high.astype(jnp.float32)).astype(jnp.bfloat16)


def product(a, b, turned=False):
    dims = (((1,), (1 if turned else 0,)), ((), ()))

    def one(x, y):
        return lax.dot_general(x, y, dims, preferred_element_type=jnp.float32)

    return one(a[0], b[0]) + one(a[0], b[1]) + one(a[1], b[0])


def each(count, body, width=256):
    def one(i, carry):
        body(pl.ds(pl.multiple_of(i * width, width), width))
        return carry

    lax.fori_loop(0, count, one, 0)


def rows_kernel(t_ref, c_ref, high_ref, low_ref, out_ref, sh, sl):
    high_ref[...], low_ref[...] = split(t_ref[...])
    sh[...], sl[...] = split(c_ref[...])

    def body(at):
        inverse = (high_ref[at, :], low_ref[at, :])
        out_ref[:, at] = product((sh[...], sl[...]), inverse, True)

    each(PIV // 256, body)


def child_rows_of(inverse, rows):
    half = jax.ShapeDtypeStruct((PIV, PIV), jnp.bfloat16)
    return pl.pallas_call(
        rows_kernel,
        out_shape=[half, half, jax.ShapeDtypeStruct(rows.shape, jnp.float32)],
        in_specs=[WHOLE] * 2,
        out_specs=[WHOLE] * 3,
        scratch_shapes=[pltpu.VMEM(rows.shape, jnp.bfloat16)] * 2,
        cost_estimate=work(2, 10),
        compiler_params=limit(32),
        name="child_rows",
    )(inverse, rows)


def load_blocks(count, where_ref, there_ref, rows_ref, got, sem):
    def copy(i):
        start = pl.multiple_of(where_ref[i] * BLK, BLK)
        return pltpu.make_async_copy(
            rows_ref.at[pl.ds(start, BLK)], got.at[pl.ds(i * BLK, BLK)], sem.at[i]
        )

    for i in range(count):
        copy(i).start()
    for i in range(count):
        copy(i).wait()

        @pl.when(there_ref[i] == 0)
        def _():
            got[i * BLK : i * BLK + BLK, :] = jnp.zeros((BLK, PIV), jnp.float32)


def lead_part_kernel(
    where_ref, there_ref, place_ref, high_ref, low_ref, own_ref, rows_ref, keep_ref, give_ref, got, sem
):
    load_blocks(5, where_ref, there_ref, rows_ref, got, sem)
    core = place_ref[3]
    half = PANEL // 2
    inverse = (high_ref[...], low_ref[...])
    half_way = product(split(got[4 * BLK :, :]), inverse, True)
    solved = product(split(half_way), inverse)
    part = product(split(got[: 4 * BLK, :]), split(solved), True)
    keep_ref[...] = own_ref[pl.ds(pl.multiple_of(core * half, half), half), :] - part[:half]
    give_ref[...] = own_ref[pl.ds(pl.multiple_of((1 - core) * half, half), half), :] - part[half:]


def top_kernel(
    where_ref, there_ref, spot_ref, place_ref, high_ref, low_ref, own_ref, rows_ref, keep_ref, give_ref, got, sem
):
    load_blocks(8, where_ref, there_ref, rows_ref, got, sem)
    solved = (high_ref[...], low_ref[...])
    at_top = place_ref[0] == 0
    for half, out_ref in ((0, keep_ref), (1, give_ref)):
        part = product(split(got[half * PANEL : half * PANEL + PANEL, :]), solved)
        for i in range(4):
            at = pl.multiple_of(spot_ref[half * 4 + i] * BLK, BLK)
            own = jnp.where(at_top, own_ref[pl.ds(at, BLK), :], 0.0)
            out_ref[i] = part[i * BLK : i * BLK + BLK] + own


def solved_kernel(where_ref, there_ref, high_ref, low_ref, rows_ref, oh_ref, ol_ref, got, sem):
    load_blocks(4, where_ref, there_ref, rows_ref, got, sem)
    inverse = (high_ref[...], low_ref[...])
    half_way = product(split(got[...]), inverse, True)
    solved = product(split(half_way), inverse)
    oh_ref[...], ol_ref[...] = split(-solved.T)


def with_blocks(kernel, count, out_shape, tables, inputs, rows):
    return pl.pallas_call(
        kernel,
        out_shape=out_shape,
        in_specs=[TABLE] * len(tables)
        + [WHOLE] * len(inputs)
        + [pl.BlockSpec(memory_space=pl.ANY)],
        out_specs=[WHOLE] * len(out_shape),
        scratch_shapes=[
            pltpu.VMEM((count * BLK, PIV), jnp.float32),
            pltpu.SemaphoreType.DMA((count,)),
        ],
        cost_estimate=work(3, 8),
        compiler_params=limit(40),
    )(*tables, *inputs, rows)


def solve_kernel(
    place_ref, t_ref, first_ref, second_ref, top_ref, *refs
):
    pieces, (out_ref, th, tl, uh, ul, ph, pl_, fh, fl, xh, xl, rh, rl) = refs[:8], refs[8:]
    g, c, px, py = place_ref[0], place_ref[1], place_ref[4], place_ref[5]
    half = PANEL

    th[...], tl[...] = split(t_ref[...])
    for i in range(4):
        for j in range(4):
            rows = slice(256 * j, 256 * j + 256)
            cols = slice(256 * i, 256 * i + 256)
            uh[rows, cols], ul[rows, cols] = split(t_ref[cols, rows].T)
    for source in range(8):
        start = (source % 2 * 4 + source // 2) * BLK
        at = slice(start, start + BLK)
        ph[at, :], pl_[at, :] = split(top_ref[source])

    for i in range(4):
        at, upto = slice(256 * i, 256 * i + 256), slice(0, 256 * i + 256)
        x = product((th[at, upto], tl[at, upto]), (ph[upto, :], pl_[upto, :]))
        fh[at, :], fl[at, :] = split(x)

    @pl.when(g == 0)
    def _():
        @pl.when(c == 0)
        def _():
            out_ref[...] = -first_ref[...]

        @pl.when(c == 1)
        def _():
            out_ref[:half, :] = jnp.zeros((half, half), jnp.float32)
            out_ref[half:, :] = -second_ref[half:, :]

        @pl.when(c >= 2)
        def _():
            out_ref[:half, :] = jnp.zeros((half, half), jnp.float32)
            left = split(first_ref[half:, :])
            out_ref[half:, :] = product(left, (fh[:half, :], fl[:half, :]))

    @pl.when(g > 0)
    def _():
        @pl.when(c == 0)
        def _():
            xh[...], xl[...] = -uh[:, :half], -ul[:, :half]

        @pl.when(c == 1)
        def _():
            xh[...], xl[...] = -uh[:, half:], -ul[:, half:]

        @pl.when(c >= 2)
        def _():
            for i in range(4):
                at, since = slice(256 * i, 256 * i + 256), slice(256 * i, LEAD)
                x = product((uh[at, since], ul[at, since]), (fh[since, :], fl[since, :]))
                xh[at, :], xl[at, :] = split(x)

        for sx in range(4):
            for sy in range(4):
                x, y = (px + 4 - sx) % 4, (py + 4 - sy) % 4
                where = x * 4 + y
                source = where // 2
                row = pl.multiple_of((where % 2) * half, half)
                column = pl.multiple_of(((source % 2) * 4 + source // 2) * BLK, BLK)
                tile = jnp.concatenate([pieces[sx][sy], pieces[4 + sy][sx]], axis=0).T
                to = (pl.ds(row, half), pl.ds(column, BLK))
                rh[to], rl[to] = split(tile)

        def update(at):
            out_ref[at, :] = product((rh[at, :], rl[at, :]), (xh[...], xl[...]))

        each(4, update)


def solve(place, inverse, first, second, top, pieces):
    def pair(rows, cols):
        return [pltpu.VMEM((rows, cols), jnp.bfloat16)] * 2

    return pl.pallas_call(
        solve_kernel,
        out_shape=jax.ShapeDtypeStruct((LEAD, PANEL), jnp.float32),
        in_specs=[TABLE] + [WHOLE] * 12,
        out_specs=WHOLE,
        scratch_shapes=pair(LEAD, LEAD) * 2 + pair(LEAD, PANEL) * 3 + pair(LEAD, LEAD),
        cost_estimate=work(10, 20),
        compiler_params=limit(36),
        name="solve",
    )(place, inverse, first, second, top, *pieces)


def schur_kernel(step_blocks, present_ref, absent_ref, rows_ref, high_ref, low_ref, out_ref, buf, zero, sem, zsem):
    step = pl.program_id(0)
    steps = pl.num_programs(0)
    slot = lax.rem(step, 2)

    def put(which, index, to):
        return pltpu.make_async_copy(
            buf.at[which, pl.ds(index * BLK, BLK)],
            out_ref.at[pl.ds(pl.multiple_of(to * BLK, BLK), BLK)],
            sem.at[which, index],
        )

    def clear(index, to):
        return pltpu.make_async_copy(
            zero, out_ref.at[pl.ds(pl.multiple_of(to * BLK, BLK), BLK)], zsem.at[index]
        )

    @pl.when(step == 0)
    def _():
        zero[...] = jnp.zeros_like(zero)

    for i in range(step_blocks):
        clear(i, absent_ref[step * step_blocks + i]).start()
    x = rows_ref[...]
    xh = x.astype(jnp.bfloat16)
    xl = (x - xh.astype(jnp.float32)).astype(jnp.bfloat16)
    wh = high_ref[...]
    total = jnp.dot(xh, wh, preferred_element_type=jnp.float32)
    total += jnp.dot(xh, low_ref[...], preferred_element_type=jnp.float32)
    total += jnp.dot(xl, wh, preferred_element_type=jnp.float32)

    @pl.when(step >= 2)
    def _():
        for i in range(step_blocks):
            put(slot, i, 0).wait()

    buf[slot] = total
    for i in range(step_blocks):
        put(slot, i, present_ref[step * step_blocks + i]).start()
    for i in range(step_blocks):
        clear(i, 0).wait()

    @pl.when(step == steps - 1)
    def _():
        for i in range(step_blocks):
            put(slot, i, 0).wait()
            put(1 - slot, i, 0).wait()


def schur_slab(present, absent, rows, high, low, step_blocks=4):
    width = high.shape[1]
    steps = SBLK // step_blocks
    return pl.pallas_call(
        functools.partial(schur_kernel, step_blocks),
        out_shape=jax.ShapeDtypeStruct((PBLK * BLK, width), jnp.float32),
        grid_spec=pltpu.PrefetchScalarGridSpec(
            num_scalar_prefetch=2,
            grid=(steps,),
            in_specs=[
                pl.BlockSpec((step_blocks * BLK, PIV), lambda i, p, a: (i, 0)),
                pl.BlockSpec((PIV, width), lambda i, p, a: (0, 0)),
                pl.BlockSpec((PIV, width), lambda i, p, a: (0, 0)),
            ],
            out_specs=pl.BlockSpec(memory_space=pltpu.HBM),
            scratch_shapes=[
                pltpu.VMEM((2, step_blocks * BLK, width), jnp.float32),
                pltpu.VMEM((BLK, width), jnp.float32),
                pltpu.SemaphoreType.DMA((2, step_blocks)),
                pltpu.SemaphoreType.DMA((step_blocks,)),
            ],
        ),
        cost_estimate=pl.CostEstimate(
            flops=6 * SBLK * BLK * PIV * width, bytes_accessed=36 << 20, transcendentals=0
        ),
        compiler_params=pltpu.CompilerParams(
            dimension_semantics=("arbitrary",), vmem_limit_bytes=58 << 20
        ),
        name="schur",
    )(present, absent, rows, high, low)


def swap_core(x):
    return lax.ppermute(x, "grp", [(i, i ^ 1) for i in range(8)])


def along_z(x, shift):
    return lax.ppermute(x, "grp", [(i, (i + 2 * shift) % 8) for i in range(8)])


def along_x(x, shift):
    return lax.ppermute(x, "col", [(i, (i + 4 * shift) % 16) for i in range(16)])


def along_y(x, shift):
    return lax.ppermute(x, "col", [(i, i // 4 * 4 + (i + shift) % 4) for i in range(16)])


def fetch(x, mover):
    return [x] + [mover(x, s) for s in (1, 2, 3)]


def plane_near(x):
    half = x.shape[0] // 2
    return jnp.stack(fetch(x[:half], along_y)), jnp.stack(fetch(x[half:], along_x))


def plane_far(near):
    return fetch(near[0], along_x) + fetch(near[1], along_y)


def pick(x, index, axis):
    return lax.dynamic_index_in_dim(x, index, axis, keepdims=False)


def after(value, *others):
    return lax.optimization_barrier((value, *others))[0]


def program(pivot_blocks, coupling, block_map, parent_matrix):
    g = lax.axis_index("grp")
    c = lax.axis_index("col")
    pz, core = g // 2, g % 2
    px, py = c // 4, c % 4
    at_top = g == 0
    place = jnp.stack([g, c, pz, core, px, py]).astype(jnp.int32)

    gathered = lax.all_gather(coupling[0], "col", axis=0, tiled=True)

    lead_own = []
    for s in range(8):
        row, column = PANEL * (s % 2), BLK * (s // 2)
        piece = parent_matrix[row : row + PANEL, column : column + BLK]
        lead_own.append(lax.ppermute(piece, ("grp", "col"), [(0, s), (1, 8 + s)]))

    mapping = pick(block_map, g, 0)
    spots = jnp.arange(PBLK, dtype=jnp.int32)
    matches = mapping[None, :] == spots[:, None]
    position = jnp.sum(jnp.where(matches, jnp.arange(SBLK, dtype=jnp.int32)[None, :], 0), axis=1)
    present = jnp.any(matches, axis=1)
    rank = jnp.sum((spots[None, :] < spots[:, None]) & ~present[None, :], axis=1)
    slots = jnp.arange(SBLK, dtype=jnp.int32)
    absent = jnp.sum(
        jnp.where((rank[None, :] == slots[:, None]) & ~present[None, :], spots[None, :], 0), axis=1
    ).astype(jnp.int32)
    n = jnp.arange(17, dtype=jnp.int32)
    side = jnp.where(n % 4 < 2, core, 1 - core)
    lead_spot = 4 * (c % 2) + 2 * side + n % 2
    top_side = jnp.where(n < 13, core, 1 - core)
    top_spot = 4 * top_side + (pz + n - 9) % 4
    spot = jnp.where(
        n < 4, lead_spot, jnp.where(n < 5, c // 2, jnp.where(n < 9, 4 * c + n - 5, top_spot))
    ).astype(jnp.int32)
    chosen = spot[:, None] == spots[None, :]
    where = jnp.sum(jnp.where(chosen, position[None, :], 0), axis=1)
    there = jnp.sum((chosen & present[None, :]).astype(jnp.int32), axis=1)

    pivot, mapping, where, there, absent, place, spot = lax.optimization_barrier(
        (pivot_blocks[0], mapping, where, there, absent, place, spot)
    )
    child_inv = child_factor(pivot)
    inv_high, inv_low, child_rows = child_rows_of(child_inv, coupling[0])
    own = lead_own[0]
    for more in lead_own[1:]:
        own = own + more
    gathered, child_rows, own = lax.optimization_barrier((gathered, child_rows, own))

    half_piece = jax.ShapeDtypeStruct((PANEL // 2, BLK), jnp.float32)
    lead_keep, lead_give = with_blocks(
        lead_part_kernel,
        5,
        [half_piece] * 2,
        (where[:5], there[:5], place),
        (inv_high, inv_low, own),
        gathered,
    )
    lead_got = swap_core(lead_give)
    wide = jax.ShapeDtypeStruct((PIV, PANEL), jnp.bfloat16)
    solved = with_blocks(
        solved_kernel, 4, [wide, wide], (where[5:9], there[5:9]), (inv_high, inv_low), gathered
    )

    half_top = jax.ShapeDtypeStruct((4, BLK, PANEL), jnp.float32)
    top_keep, top_give = with_blocks(
        top_kernel,
        8,
        [half_top] * 2,
        (where[9:], there[9:], spot[9:], place),
        (*solved, parent_matrix),
        gathered,
    )
    top_got = swap_core(top_give)
    lead_mine = after(lead_keep + lead_got, top_give)
    others = [along_z(lead_mine, s) for s in (1, 2, 3)]
    top_mine = top_keep + top_got
    strips = [along_z(top_mine[s], s) for s in (1, 2, 3)]
    lead_mine = lead_mine + others[0] + others[1] + others[2]
    lead_other = swap_core(lead_mine)
    lead_near = (
        jnp.stack(fetch(lead_mine, along_y)),
        jnp.stack(fetch(lead_other, along_x)),
    )
    strip = top_mine[0] + strips[0] + strips[1] + strips[2]
    turn = [
        (gg * 16 + cc, (cc // 2) * 16 + 2 * gg + cc % 2) for gg in range(8) for cc in range(16)
    ]
    turned = lax.ppermute(strip, ("grp", "col"), turn)
    top_all = lax.all_gather(strip, "grp", axis=0)

    slab_all = schur_slab(mapping, absent, after(gathered, strip), *solved)
    update = lax.psum_scatter(slab_all, "grp", scatter_dimension=0, tiled=True)

    lead_far = plane_far(lead_near)
    turned, _, top_all = lax.optimization_barrier((turned, slab_all, top_all))
    row_near = plane_near(turned)
    inv, low_first = lead_start(place, lead_far, 4)
    row_far = plane_far(row_near)
    inv, low_second = lead_next(inv, 4, 8)

    change = solve(place, inv, low_first, low_second, top_all, row_far)

    below = (g > 0) & (c >= 2)
    keep_first = below | (at_top & (c > 0))
    keep_second = c >= 2
    kept = jnp.where(jnp.arange(LEAD)[:, None] < PANEL, keep_first, keep_second)
    base = jnp.where(kept, parent_matrix, 0.0) - change
    matrix = lax.optimization_barrier(base) + jnp.where(kept, update, 0.0)
    return (child_rows[None], matrix)


def solution(mesh):
    return jax.shard_map(
        program,
        mesh=mesh,
        in_specs=(P("grp", None, None), P("grp", "col", None), P(), P("grp", "col")),
        out_specs=(P("grp", "col", None), P("grp", "col")),
        check_vma=False,
    )
```

profile of v0, /device:TPU:39, one launch (start us, length us, event | category | flops | bytes accessed | tf_op | source)
XLA Modules:
  0.0 362.5 jit_solution(1592752645707827373)
XLA Ops:
  8.0 2.4 fusion.14
  17.4 2.2 copy-done.12
  19.6 46.9 %child_factor.1.t_ref = f32[1024,1024]{1,0:T(8,128)S(1)} custom-call(f32[1024,1024]{1,0:T(8,128)S(1)} %bitcast.50), custom_call_target="tpu_custom_call" | custom-call | flops 40000000000 | bytes 12582912 | tf_op jit(solution)/shard_map/child_factor/pallas_call | solution.py:180
  66.9 4.4 %child_rows.1 = (bf16[1024,1024]{1,0:T(8,128)(2,1)S(1)}, bf16[1024,1024]{1,0:T(8,128)(2,1)S(1)}, f32[256,1024]{1,0:T(8,128)}) custom-call(f32[1024,1024]{1,0:T(8,128)S(1)} %child_factor.1.t_ref, f32[256,1024]{1,0:T(8,128)S(1)} %bitcast.47), custom_call_target="tpu_custom_call" | custom-call | flops 2000000000 | bytes 10485760 | tf_op jit(solution)/shard_map/child_rows/pallas_call | solution.py:250
  74.1 51.1 %all-gather.5.cloned.1.call-done = f32[1,4096,1024]{2,1,0:T(8,128)} async-done(((f32[1,256,1024]{2,1,0:T(8,128)}), f32[1,4096,1024]{2,1,0:T(8,128)}) %all-gather.5.cloned.1.call-update) | async-done | bytes 16777232 | tf_op jit(solution)/shard_map/all_gather | solution.py:548
  128.4 9.3 %shard_map.60 = (bf16[1024,512]{1,0:T(8,128)(2,1)S(1)}, bf16[1024,512]{1,0:T(8,128)(2,1)S(1)}) custom-call(s32[4]{0:T(128)S(1)} %slice.76.where_ref, s32[4]{0:T(128)S(1)} %slice.77.there_ref, bf16[1024,1024]{1,0:T(8,128)(2,1)S(1)} %copy-done.4, bf16[1024,1024]{1,0:T(8,128)(2,1)S(1)} %copy-done.7, f32[4096,1024]{1,0:T(8,128)} %bitcast.52), custom_call_target="tpu_custom_call" | custom-call | flops 3000000000 | bytes 8388608 | tf_op jit(solution)/shard_map/pallas_call | solution.py:316
  137.7 6.4 %shard_map.61 = (f32[4,128,512]{2,1,0:T(8,128)S(1)}, f32[4,128,512]{2,1,0:T(8,128)S(1)}) custom-call(s32[8]{0:T(128)S(1)} %slice.73.where_ref, s32[8]{0:T(128)S(1)} %slice.74.there_ref, s32[8]{0:T(128)S(1)} %slice.75.spot_ref, s32[6]{0:T(128)S(1)} %stack.87.place_ref, bf16[1024,512]{1,0:T(8,128)(2,1)S(1)} %get-tuple-element.42.high_ref, ...), custom_call_target="tpu_custom_call" | custom-call | flops 3000000000 | bytes 8388608 | tf_op jit(solution)/shard_map/pallas_call | solution.py:316
  145.4 2.3 collective-permute-done.25
  151.3 4.2 %collective-permute-done.26 = f32[128,512]{1,0:T(8,128)S(1)} collective-permute-done((f32[128,512]{1,0:T(8,128)S(1)}, f32[128,512]{1,0:T(8,128)S(1)}, u32[]{:S(2)}, u32[]{:S(2)}) %collective-permute-start.26) | collective-permute-done | bytes 262176 | tf_op jit(solution)/shard_map/ppermute | solution.py:508
  156.5 6.1 %collective-permute-done.27 = f32[128,512]{1,0:T(8,128)S(1)} collective-permute-done((f32[128,512]{1,0:T(8,128)S(1)}, f32[128,512]{1,0:T(8,128)S(1)}, u32[]{:S(2)}, u32[]{:S(2)}) %collective-permute-start.27) | collective-permute-done | bytes 262176 | tf_op jit(solution)/shard_map/ppermute | solution.py:508
  163.5 23.0 %schur.1 = f32[8192,512]{1,0:T(8,128)} custom-call(s32[32]{0:T(128)} %copy-done.20, s32[32]{0:T(128)} %select_reduce_fusion.absent_ref, f32[4096,1024]{1,0:T(8,128)} %bitcast.54, bf16[1024,512]{1,0:T(8,128)(2,1)} %copy-done.10, bf16[1024,512]{1,0:T(8,128)(2,1)} %copy-done.11), custom_call_target="tpu_custom_call" | custom-call | flops 12884901888 | bytes 37748736 | tf_op jit(solution)/shard_map/schur/pallas_call | solution.py:474
  189.7 6.7 %shard_map.59 = (f32[256,128]{1,0:T(8,128)S(1)}, f32[256,128]{1,0:T(8,128)S(1)}) custom-call(s32[5]{0:T(128)S(1)} %bitcast.49, s32[5]{0:T(128)S(1)} %bitcast.48, s32[6]{0:T(128)S(1)} %stack.87.place_ref, bf16[1024,1024]{1,0:T(8,128)(2,1)S(1)} %copy-done.5, bf16[1024,1024]{1,0:T(8,128)(2,1)S(1)} %copy-done.8, f32[512,128]{1,0:T(8,128)S(1)} %add_add_fusion.own_ref, ...), custom_call_target="tpu_custom_call" | custom-call | flops 3000000000 | bytes 8388608 | tf_op jit(solution)/shard_map/pallas_call | solution.py:316
  200.7 2.0 collective-permute-start.9
  202.7 2.7 collective-permute-done.11
  205.4 3.3 collective-permute-done.10
  208.7 3.2 collective-permute-done.9
  214.0 9.0 %collective-permute-start.29 = (f32[128,512]{1,0:T(8,128)S(1)}, f32[128,512]{1,0:T(8,128)S(1)}, u32[]{:S(2)}, u32[]{:S(2)}) collective-permute-start(f32[128,512]{1,0:T(8,128)S(1)} %copy-done.14), channel_id=1, source_target_pairs={{0,0},{1,1},{2,16},{3,17},{4,32},{5,33},{6,48},{7,49},{8,64},{9,65... | collective-permute-start | bytes 786440 | tf_op jit(solution)/shard_map/ppermute | solution.py:627
  225.7 2.7 collective-permute-start.20
  229.4 3.4 collective-permute-done.29
  233.0 12.2 %collective-permute-done.21 = f32[256,128]{1,0:T(8,128)S(1)} collective-permute-done((f32[256,128]{1,0:T(8,128)S(1)}, f32[256,128]{1,0:T(8,128)S(1)}, u32[]{:S(2)}, u32[]{:S(2)}) %collective-permute-start.21) | collective-permute-done | bytes 131104 | tf_op jit(solution)/shard_map/ppermute | solution.py:512
  247.9 5.4 %collective-permute-start.16 = (f32[4,256,128]{2,1,0:T(8,128)S(1)}, f32[4,256,128]{2,1,0:T(8,128)}, u32[]{:S(2)}, u32[]{:S(2)}) collective-permute-start(f32[4,256,128]{2,1,0:T(8,128)S(1)} %pad_maximum_fusion.refs_0_), channel_id=1, source_target_pairs={{0,8},{1,9},{2,10},{3,11},{4,12},{5,13},{6,14},{7,15},{8,0},{9,1},... | collective-permute-start | bytes 1572872 | tf_op jit(solution)/shard_map/ppermute | solution.py:512
  258.7 6.5 %collective-permute-done.16.refs_2_ = f32[4,256,128]{2,1,0:T(8,128)} collective-permute-done((f32[4,256,128]{2,1,0:T(8,128)S(1)}, f32[4,256,128]{2,1,0:T(8,128)}, u32[]{:S(2)}, u32[]{:S(2)}) %collective-permute-start.16) | collective-permute-done | bytes 524320 | tf_op jit(solution)/shard_map/ppermute | solution.py:512
  265.2 3.2 collective-permute-start.37
  268.4 5.6 %collective-permute-done.15.refs_1_ = f32[4,256,128]{2,1,0:T(8,128)} collective-permute-done((f32[4,256,128]{2,1,0:T(8,128)S(1)}, f32[4,256,128]{2,1,0:T(8,128)}, u32[]{:S(2)}, u32[]{:S(2)}) %collective-permute-start.15) | collective-permute-done | bytes 524320 | tf_op jit(solution)/shard_map/ppermute | solution.py:512
  274.1 2.3 collective-permute-start.36
  278.7 2.9 collective-permute-done.22.refs_5_
  281.6 26.5 %shard_map.62 = (f32[1024,1024]{1,0:T(8,128)S(1)}, f32[1024,512]{1,0:T(8,128)S(1)}) custom-call(s32[6]{0:T(128)S(1)} %stack.87.place_ref, f32[4,256,128]{2,1,0:T(8,128)S(1)} %pad_maximum_fusion.refs_0_, f32[4,256,128]{2,1,0:T(8,128)} %collective-permute-done.15.refs_1_, f32[4,256,128]{2,1,0:T(8,128)} %collective-permute-done.16.refs_2_, ...), custom_call_target="tpu_custom_call" | custom-call | flops 10000000000 | bytes 12582912 | tf_op jit(solution)/shard_map/pallas_call | solution.py:207
  309.1 2.8 collective-permute-start.33
  314.6 21.0 %shard_map.63 = (f32[1024,1024]{1,0:T(8,128)S(1)}, f32[1024,512]{1,0:T(8,128)S(1)}) custom-call(f32[1024,1024]{1,0:T(8,128)S(1)} %get-tuple-element.46.t_in), custom_call_target="tpu_custom_call" | custom-call | flops 10000000000 | bytes 12582912 | tf_op jit(solution)/shard_map/pallas_call | solution.py:212
  335.6 4.0 %collective-permute-done.39.refs_5_ = f32[4,64,512]{2,1,0:T(8,128)S(1)} collective-permute-done((f32[4,64,512]{2,1,0:T(8,128)S(1)}, f32[4,64,512]{2,1,0:T(8,128)S(1)}, u32[]{:S(2)}, u32[]{:S(2)}) %collective-permute-start.39) | collective-permute-done | bytes 524320 | tf_op jit(solution)/shard_map/ppermute | solution.py:516
  339.6 10.7 %solve.1 = f32[1024,512]{1,0:T(8,128)S(1)} custom-call(s32[6]{0:T(128)S(1)} %stack.87.place_ref, f32[1024,1024]{1,0:T(8,128)S(1)} %get-tuple-element.47.t_ref, f32[1024,512]{1,0:T(8,128)S(1)} %get-tuple-element.48.first_ref, f32[1024,512]{1,0:T(8,128)S(1)} %get-tuple-element.49.second_ref, f32[8,128,512]{2,1,0:T(8,128)S(1)} %bitcast.51, ...), custom_call_target="tpu_custom_call" | custom-call | flops 10000000000 | bytes 20971520 | tf_op jit(solution)/shard_map/solve/pallas_call | solution.py:410
  352.0 3.8 %select_add_fusion = f32[1024,512]{1,0:T(8,128)} fusion(f32[1024,512]{1,0:T(8,128)} %select_subtract_fusion, f32[1024,512]{1,0:T(8,128)} %reduce-scatter.2.cloned.1.call-done, pred[1024]{0:T(1024)(128)(4,1)S(1)} %fusion.7), kind=kLoop, calls=%fused_computation | loop fusion | flops 1048576 | bytes 6292480 | tf_op jit(solution)/shard_map/add | solution.py:647
  (141 shorter events, 49.6 us)
Async XLA Ops:
  7.2 118.0 %all-gather.5.cloned.1.call-start = ((), (), s32[]{:S(2)}) async-start(), calls=%async_computation.2 | async-start | bytes 17825792 | tf_op jit(solution)/shard_map/all_gather | solution.py:548
  7.9 224.9 %all-gather.7.cloned.1.call-start = ((), (), s32[]{:S(2)}) async-start(), calls=%async_computation.3 | async-start | bytes 2359296 | tf_op jit(solution)/shard_map/all_gather | solution.py:628
  12.4 61.5 %collective-permute-start.5 = (f32[512,128]{1,0:T(8,128)}, f32[512,128]{1,0:T(8,128)S(1)}, u32[]{:S(2)}, u32[]{:S(2)}) collective-permute-start(f32[512,128]{1,0:T(8,128)} %get-tuple-element.61), channel_id=1, source_target_pairs={{0,5},{1,13}} | collective-permute-start | bytes 786440 | tf_op jit(solution)/shard_map/ppermute | solution.py:554
  13.1 60.9 %collective-permute-start.4 = (f32[512,128]{1,0:T(8,128)S(1)}, f32[512,128]{1,0:T(8,128)S(1)}, u32[]{:S(2)}, u32[]{:S(2)}) collective-permute-start(f32[512,128]{1,0:T(8,128)S(1)} %get-tuple-element.62), channel_id=1, source_target_pairs={{0,4},{1,12}} | collective-permute-start | bytes 786440 | tf_op jit(solution)/shard_map/ppermute | solution.py:554
  15.2 58.8 %collective-permute-start.3 = (f32[512,128]{1,0:T(8,128)S(1)}, f32[512,128]{1,0:T(8,128)S(1)}, u32[]{:S(2)}, u32[]{:S(2)}) collective-permute-start(f32[512,128]{1,0:T(8,128)S(1)} %get-tuple-element.63), channel_id=1, source_target_pairs={{0,3},{1,11}} | collective-permute-start | bytes 786440 | tf_op jit(solution)/shard_map/ppermute | solution.py:554
  15.9 58.1 %collective-permute-start.2 = (f32[512,128]{1,0:T(8,128)S(1)}, f32[512,128]{1,0:T(8,128)S(1)}, u32[]{:S(2)}, u32[]{:S(2)}) collective-permute-start(f32[512,128]{1,0:T(8,128)S(1)} %get-tuple-element.64), channel_id=1, source_target_pairs={{0,2},{1,10}} | collective-permute-start | bytes 786440 | tf_op jit(solution)/shard_map/ppermute | solution.py:554
  16.6 57.4 %collective-permute-start = (f32[512,128]{1,0:T(8,128)S(1)}, f32[512,128]{1,0:T(8,128)S(1)}, u32[]{:S(2)}, u32[]{:S(2)}) collective-permute-start(f32[512,128]{1,0:T(8,128)S(1)} %get-tuple-element.65), channel_id=1, source_target_pairs={{0,0},{1,8}} | collective-permute-start | bytes 786440 | tf_op jit(solution)/shard_map/ppermute | solution.py:554
  149.5 13.2 %collective-permute-start.27 = (f32[128,512]{1,0:T(8,128)S(1)}, f32[128,512]{1,0:T(8,128)S(1)}, u32[]{:S(2)}, u32[]{:S(2)}) collective-permute-start(f32[128,512]{1,0:T(8,128)S(1)} %get-tuple-element.68), channel_id=1, source_target_pairs={{0,64},{16,80},{32,96},{48,112},{64,0},{80,16},{96,32},{112,48},{1... | collective-permute-start | bytes 786440 | tf_op jit(solution)/shard_map/ppermute | solution.py:508
  163.4 188.5 %reduce-scatter.2.cloned.1.call-start = ((), (), s32[]{:S(2)}) async-start(), calls=%async_computation.1 | async-start | bytes 18874368 | tf_op jit(solution)/shard_map/reduce_scatter | solution.py:631
  200.7 11.2 %collective-permute-start.9 = (f32[256,128]{1,0:T(8,128)S(1)}, f32[256,128]{1,0:T(8,128)S(1)}, u32[]{:S(2)}, u32[]{:S(2)}) collective-permute-start(f32[256,128]{1,0:T(8,128)S(1)} %add.169), channel_id=1, source_target_pairs={{0,32},{16,48},{32,64},{48,80},{64,96},{80,112},{96,0},{112,16},{1... | collective-permute-start | bytes 393224 | tf_op jit(solution)/shard_map/ppermute | solution.py:508
  212.0 11.1 %collective-permute-start.14 = (f32[256,128]{1,0:T(8,128)S(1)}, f32[256,128]{1,0:T(8,128)S(1)}, u32[]{:S(2)}, u32[]{:S(2)}) collective-permute-start(f32[256,128]{1,0:T(8,128)S(1)} %add_add_fusion.1), channel_id=1, source_target_pairs={{0,3},{1,0},{2,1},{3,2},{4,7},{5,4},{6,5},{7,6},{8,11},{9,8},{10,9... | collective-permute-start | bytes 393224 | tf_op jit(solution)/shard_map/ppermute | solution.py:516
  212.3 10.8 %collective-permute-start.13 = (f32[256,128]{1,0:T(8,128)S(1)}, f32[256,128]{1,0:T(8,128)S(1)}, u32[]{:S(2)}, u32[]{:S(2)}) collective-permute-start(f32[256,128]{1,0:T(8,128)S(1)} %add_add_fusion.1), channel_id=1, source_target_pairs={{0,2},{1,3},{2,0},{3,1},{4,6},{5,7},{6,4},{7,5},{8,10},{9,11},{10,... | collective-permute-start | bytes 393224 | tf_op jit(solution)/shard_map/ppermute | solution.py:516
  214.0 18.8 %collective-permute-start.29 = (f32[128,512]{1,0:T(8,128)S(1)}, f32[128,512]{1,0:T(8,128)S(1)}, u32[]{:S(2)}, u32[]{:S(2)}) collective-permute-start(f32[128,512]{1,0:T(8,128)S(1)} %copy-done.14), channel_id=1, source_target_pairs={{0,0},{1,1},{2,16},{3,17},{4,32},{5,33},{6,48},{7,49},{8,64},{9,65... | collective-permute-start | bytes 786440 | tf_op jit(solution)/shard_map/ppermute | solution.py:627
  223.2 31.5 %collective-permute-start.17 = (f32[4,256,128]{2,1,0:T(8,128)S(1)}, f32[4,256,128]{2,1,0:T(8,128)}, u32[]{:S(2)}, u32[]{:S(2)}) collective-permute-start(f32[4,256,128]{2,1,0:T(8,128)S(1)} %pad_maximum_fusion.refs_0_), channel_id=1, source_target_pairs={{0,12},{1,13},{2,14},{3,15},{4,0},{5,1},{6,2},{7,3},{8,4},{9,5},{1... | collective-permute-start | bytes 1572872 | tf_op jit(solution)/shard_map/ppermute | solution.py:512
  224.8 20.4 %collective-permute-start.21 = (f32[256,128]{1,0:T(8,128)S(1)}, f32[256,128]{1,0:T(8,128)S(1)}, u32[]{:S(2)}, u32[]{:S(2)}) collective-permute-start(f32[256,128]{1,0:T(8,128)S(1)} %collective-permute-done.18), channel_id=1, source_target_pairs={{0,12},{1,13},{2,14},{3,15},{4,0},{5,1},{6,2},{7,3},{8,4},{9,5},{1... | collective-permute-start | bytes 393224 | tf_op jit(solution)/shard_map/ppermute | solution.py:512
  225.7 20.9 %collective-permute-start.20 = (f32[256,128]{1,0:T(8,128)S(1)}, f32[256,128]{1,0:T(8,128)}, u32[]{:S(2)}, u32[]{:S(2)}) collective-permute-start(f32[256,128]{1,0:T(8,128)S(1)} %collective-permute-done.18), channel_id=1, source_target_pairs={{0,8},{1,9},{2,10},{3,11},{4,12},{5,13},{6,14},{7,15},{8,0},{9,1},... | collective-permute-start | bytes 393224 | tf_op jit(solution)/shard_map/ppermute | solution.py:512
  228.4 19.5 %collective-permute-start.19 = (f32[256,128]{1,0:T(8,128)S(1)}, f32[256,128]{1,0:T(8,128)}, u32[]{:S(2)}, u32[]{:S(2)}) collective-permute-start(f32[256,128]{1,0:T(8,128)S(1)} %collective-permute-done.18), channel_id=1, source_target_pairs={{0,4},{1,5},{2,6},{3,7},{4,8},{5,9},{6,10},{7,11},{8,12},{9,13},{1... | collective-permute-start | bytes 393224 | tf_op jit(solution)/shard_map/ppermute | solution.py:512
  232.9 21.8 %collective-permute-start.31 = (f32[64,512]{1,0:T(8,128)S(1)}, f32[64,512]{1,0:T(8,128)S(1)}, u32[]{:S(2)}, u32[]{:S(2)}) collective-permute-start(f32[64,512]{1,0:T(8,128)S(1)} %get-tuple-element.72), channel_id=1, source_target_pairs={{0,2},{1,3},{2,0},{3,1},{4,6},{5,7},{6,4},{7,5},{8,10},{9,11},{10,... | collective-permute-start | bytes 393224 | tf_op jit(solution)/shard_map/ppermute | solution.py:516
  247.9 17.3 %collective-permute-start.16 = (f32[4,256,128]{2,1,0:T(8,128)S(1)}, f32[4,256,128]{2,1,0:T(8,128)}, u32[]{:S(2)}, u32[]{:S(2)}) collective-permute-start(f32[4,256,128]{2,1,0:T(8,128)S(1)} %pad_maximum_fusion.refs_0_), channel_id=1, source_target_pairs={{0,8},{1,9},{2,10},{3,11},{4,12},{5,13},{6,14},{7,15},{8,0},{9,1},... | collective-permute-start | bytes 1572872 | tf_op jit(solution)/shard_map/ppermute | solution.py:512
  254.7 19.4 %collective-permute-start.15 = (f32[4,256,128]{2,1,0:T(8,128)S(1)}, f32[4,256,128]{2,1,0:T(8,128)}, u32[]{:S(2)}, u32[]{:S(2)}) collective-permute-start(f32[4,256,128]{2,1,0:T(8,128)S(1)} %pad_maximum_fusion.refs_0_), channel_id=1, source_target_pairs={{0,4},{1,5},{2,6},{3,7},{4,8},{5,9},{6,10},{7,11},{8,12},{9,13},{1... | collective-permute-start | bytes 1572872 | tf_op jit(solution)/shard_map/ppermute | solution.py:512
  254.8 21.6 %collective-permute-start.24 = (f32[4,256,128]{2,1,0:T(8,128)S(1)}, f32[4,256,128]{2,1,0:T(8,128)}, u32[]{:S(2)}, u32[]{:S(2)}) collective-permute-start(f32[4,256,128]{2,1,0:T(8,128)S(1)} %pad_maximum_fusion.1.refs_4_), channel_id=1, source_target_pairs={{0,3},{1,0},{2,1},{3,2},{4,7},{5,4},{6,5},{7,6},{8,11},{9,8},{10,9... | collective-permute-start | bytes 1572872 | tf_op jit(solution)/shard_map/ppermute | solution.py:516
  254.9 22.2 %collective-permute-start.23 = (f32[4,256,128]{2,1,0:T(8,128)S(1)}, f32[4,256,128]{2,1,0:T(8,128)}, u32[]{:S(2)}, u32[]{:S(2)}) collective-permute-start(f32[4,256,128]{2,1,0:T(8,128)S(1)} %pad_maximum_fusion.1.refs_4_), channel_id=1, source_target_pairs={{0,2},{1,3},{2,0},{3,1},{4,6},{5,7},{6,4},{7,5},{8,10},{9,11},{10,... | collective-permute-start | bytes 1572872 | tf_op jit(solution)/shard_map/ppermute | solution.py:516
  257.2 24.4 %collective-permute-start.22 = (f32[4,256,128]{2,1,0:T(8,128)S(1)}, f32[4,256,128]{2,1,0:T(8,128)}, u32[]{:S(2)}, u32[]{:S(2)}) collective-permute-start(f32[4,256,128]{2,1,0:T(8,128)S(1)} %pad_maximum_fusion.1.refs_4_), channel_id=1, source_target_pairs={{0,1},{1,2},{2,3},{3,0},{4,5},{5,6},{6,7},{7,4},{8,9},{9,10},{10,1... | collective-permute-start | bytes 1572872 | tf_op jit(solution)/shard_map/ppermute | solution.py:516
  265.2 44.0 %collective-permute-start.37 = (f32[64,512]{1,0:T(8,128)S(1)}, f32[64,512]{1,0:T(8,128)S(1)}, u32[]{:S(2)}, u32[]{:S(2)}) collective-permute-start(f32[64,512]{1,0:T(8,128)S(1)} %get-tuple-element.71), channel_id=1, source_target_pairs={{0,8},{1,9},{2,10},{3,11},{4,12},{5,13},{6,14},{7,15},{8,0},{9,1},... | collective-permute-start | bytes 393224 | tf_op jit(solution)/shard_map/ppermute | solution.py:512
  274.1 37.9 %collective-permute-start.36 = (f32[64,512]{1,0:T(8,128)S(1)}, f32[64,512]{1,0:T(8,128)S(1)}, u32[]{:S(2)}, u32[]{:S(2)}) collective-permute-start(f32[64,512]{1,0:T(8,128)S(1)} %get-tuple-element.71), channel_id=1, source_target_pairs={{0,4},{1,5},{2,6},{3,7},{4,8},{5,9},{6,10},{7,11},{8,12},{9,13},{1... | collective-permute-start | bytes 393224 | tf_op jit(solution)/shard_map/ppermute | solution.py:512
  276.4 35.6 %collective-permute-start.38 = (f32[64,512]{1,0:T(8,128)S(1)}, f32[64,512]{1,0:T(8,128)S(1)}, u32[]{:S(2)}, u32[]{:S(2)}) collective-permute-start(f32[64,512]{1,0:T(8,128)S(1)} %get-tuple-element.71), channel_id=1, source_target_pairs={{0,12},{1,13},{2,14},{3,15},{4,0},{5,1},{6,2},{7,3},{8,4},{9,5},{1... | collective-permute-start | bytes 393224 | tf_op jit(solution)/shard_map/ppermute | solution.py:512
  277.1 36.7 %collective-permute-start.35 = (f32[4,64,512]{2,1,0:T(8,128)S(1)}, f32[4,64,512]{2,1,0:T(8,128)S(1)}, u32[]{:S(2)}, u32[]{:S(2)}) collective-permute-start(f32[4,64,512]{2,1,0:T(8,128)S(1)} %pad_maximum_fusion.2.refs_0_), channel_id=1, source_target_pairs={{0,12},{1,13},{2,14},{3,15},{4,0},{5,1},{6,2},{7,3},{8,4},{9,5},{1... | collective-permute-start | bytes 1572872 | tf_op jit(solution)/shard_map/ppermute | solution.py:512
  308.2 27.4 %collective-permute-start.34 = (f32[4,64,512]{2,1,0:T(8,128)S(1)}, f32[4,64,512]{2,1,0:T(8,128)S(1)}, u32[]{:S(2)}, u32[]{:S(2)}) collective-permute-start(f32[4,64,512]{2,1,0:T(8,128)S(1)} %pad_maximum_fusion.2.refs_0_), channel_id=1, source_target_pairs={{0,8},{1,9},{2,10},{3,11},{4,12},{5,13},{6,14},{7,15},{8,0},{9,1},... | collective-permute-start | bytes 1572872 | tf_op jit(solution)/shard_map/ppermute | solution.py:512
  309.1 26.4 %collective-permute-start.33 = (f32[4,64,512]{2,1,0:T(8,128)S(1)}, f32[4,64,512]{2,1,0:T(8,128)S(1)}, u32[]{:S(2)}, u32[]{:S(2)}) collective-permute-start(f32[4,64,512]{2,1,0:T(8,128)S(1)} %pad_maximum_fusion.2.refs_0_), channel_id=1, source_target_pairs={{0,4},{1,5},{2,6},{3,7},{4,8},{5,9},{6,10},{7,11},{8,12},{9,13},{1... | collective-permute-start | bytes 1572872 | tf_op jit(solution)/shard_map/ppermute | solution.py:512
  312.0 23.6 %collective-permute-start.41 = (f32[4,64,512]{2,1,0:T(8,128)S(1)}, f32[4,64,512]{2,1,0:T(8,128)S(1)}, u32[]{:S(2)}, u32[]{:S(2)}) collective-permute-start(f32[4,64,512]{2,1,0:T(8,128)S(1)} %pad_maximum_fusion.3.refs_4_), channel_id=1, source_target_pairs={{0,3},{1,0},{2,1},{3,2},{4,7},{5,4},{6,5},{7,6},{8,11},{9,8},{10,9... | collective-permute-start | bytes 1572872 | tf_op jit(solution)/shard_map/ppermute | solution.py:516
  313.1 22.5 %collective-permute-start.40 = (f32[4,64,512]{2,1,0:T(8,128)S(1)}, f32[4,64,512]{2,1,0:T(8,128)S(1)}, u32[]{:S(2)}, u32[]{:S(2)}) collective-permute-start(f32[4,64,512]{2,1,0:T(8,128)S(1)} %pad_maximum_fusion.3.refs_4_), channel_id=1, source_target_pairs={{0,2},{1,3},{2,0},{3,1},{4,6},{5,7},{6,4},{7,5},{8,10},{9,11},{10,... | collective-permute-start | bytes 1572872 | tf_op jit(solution)/shard_map/ppermute | solution.py:516
  313.8 25.8 %collective-permute-start.39 = (f32[4,64,512]{2,1,0:T(8,128)S(1)}, f32[4,64,512]{2,1,0:T(8,128)S(1)}, u32[]{:S(2)}, u32[]{:S(2)}) collective-permute-start(f32[4,64,512]{2,1,0:T(8,128)S(1)} %pad_maximum_fusion.3.refs_4_), channel_id=1, source_target_pairs={{0,1},{1,2},{2,3},{3,0},{4,5},{5,6},{6,7},{7,4},{8,9},{9,10},{10,1... | collective-permute-start | bytes 1572872 | tf_op jit(solution)/shard_map/ppermute | solution.py:516
  (34 other events, 319.9 us)
Sparse Core Ops, SparseCore 0:
  10.1 115.0 all-gather.4
  163.6 24.2 all-gather.6
  190.3 103.1 reduce-scatter.1
where the time goes:
time: 369 us; the launch traced here: 363 us
  Pallas kernels  155 us (42%)
  waiting for transfers between devices  113 us (31%)
  starting transfers between devices  55.1 us (15%)
  local copies, waits for them, and re-layouts  14.8 us (4%)
  between operations  14.5 us (4%)
  other arithmetic  10.3 us (3%)
    all_gather x1, waiting for transfers between devices, program(): gathered = lax.all_gather(coupling[0], 'col', axis=0, tiled=True)  51.1 us
    pallas_call x1, Pallas kernels, child_factor(): pl.pallas_call(child_kernel, out_shape=square(PIV), in_specs=[WHOLE], out...  46.9 us
    pallas_call x1, Pallas kernels, lead_start(): return lead_call(kernel, last * BLK, [TABLE] + [WHOLE] * 8)(place, *pieces)  26.5 us
    ppermute x12, waiting for transfers between devices, along_x(): lax.ppermute(x, 'col', [(i, (i + 4 * shift) % 16) for i in range(16)])  25.8 us
    pallas_call x1, Pallas kernels, schur_slab(): pl.pallas_call(functools.partial(schur_kernel, step_blocks), out_shape=ja...  23 us
    pallas_call x3, Pallas kernels, with_blocks(): pl.pallas_call(kernel, out_shape=out_shape, in_specs=[TABLE] * len(tables...  22.3 us
    ppermute x12, starting transfers between devices, along_x(): lax.ppermute(x, 'col', [(i, (i + 4 * shift) % 16) for i in range(16)])  21.8 us
    pallas_call x1, Pallas kernels, lead_next(): return lead_call(kernel, (last - first) * BLK, [WHOLE])(t)  21 us
  transfers between devices with their start and end apart: 45, of which 17 were waited for; matrix products, arithmetic and copies ran while one was open for 2% of the time, Pallas kernels for 38%

commit v1 on v0

--- a/solution.py
+++ b/solution.py
@@ -610,7 +610,7 @@
         gathered,
     )
     top_got = swap_core(top_give)
-    lead_mine = after(lead_keep + lead_got, top_give)
+    lead_mine = lead_keep + lead_got
     others = [along_z(lead_mine, s) for s in (1, 2, 3)]
     top_mine = top_keep + top_got
     strips = [along_z(top_mine[s], s) for s in (1, 2, 3)]
@@ -630,8 +630,8 @@
     slab_all = schur_slab(mapping, absent, after(gathered, strip), *solved)
     update = lax.psum_scatter(slab_all, "grp", scatter_dimension=0, tiled=True)
 
-    lead_far = plane_far(lead_near)
-    turned, _, top_all = lax.optimization_barrier((turned, slab_all, top_all))
+    near_a, near_b, _, top_all = lax.optimization_barrier((*lead_near, slab_all, top_all))
+    lead_far = plane_far((near_a, near_b))
     row_near = plane_near(turned)
     inv, low_first = lead_start(place, lead_far, 4)
     row_far = plane_far(row_near)
@@ -643,8 +643,7 @@
     keep_first = below | (at_top & (c > 0))
     keep_second = c >= 2
     kept = jnp.where(jnp.arange(LEAD)[:, None] < PANEL, keep_first, keep_second)
-    base = jnp.where(kept, parent_matrix, 0.0) - change
-    matrix = lax.optimization_barrier(base) + jnp.where(kept, update, 0.0)
+    matrix = jnp.where(kept, after(parent_matrix, change) + update, 0.0) - change
     return (child_rows[None], matrix)
 
 

time: 369 us -> 365 us (0.989)
  the two profiles are of different devices: /device:TPU:39 before, /device:TPU:114 now
where the time goes in v1:
time: 365 us; the launch traced here: 359 us
  Pallas kernels  156 us (43%)
  waiting for transfers between devices  97.5 us (27%)
  starting transfers between devices  65 us (18%)
  local copies, waits for them, and re-layouts  17.3 us (5%)
  between operations  14.5 us (4%)
  other arithmetic  8.62 us (2%)
    all_gather x1, waiting for transfers between devices, program(): gathered = lax.all_gather(coupling[0], 'col', axis=0, tiled=True)  49.4 us
    pallas_call x1, Pallas kernels, child_factor(): pl.pallas_call(child_kernel, out_shape=square(PIV), in_specs=[WHOLE], out...  46.9 us
    pallas_call x1, Pallas kernels, lead_start(): return lead_call(kernel, last * BLK, [TABLE] + [WHOLE] * 8)(place, *pieces)  26.3 us
    ppermute x12, starting transfers between devices, along_x(): lax.ppermute(x, 'col', [(i, (i + 4 * shift) % 16) for i in range(16)])  26.1 us
    pallas_call x3, Pallas kernels, with_blocks(): pl.pallas_call(kernel, out_shape=out_shape, in_specs=[TABLE] * len(tables...  23.2 us
    pallas_call x1, Pallas kernels, schur_slab(): pl.pallas_call(functools.partial(schur_kernel, step_blocks), out_shape=ja...  23.2 us
    pallas_call x1, Pallas kernels, lead_next(): return lead_call(kernel, (last - first) * BLK, [WHOLE])(t)  21 us
    ppermute x6, waiting for transfers between devices, along_z(): return lax.ppermute(x, 'grp', [(i, (i + 2 * shift) % 8) for i in range(8)])  20.7 us
  transfers between devices with their start and end apart: 45, of which 15 were waited for; matrix products, arithmetic and copies ran while one was open for 2% of the time, Pallas kernels for 39%

profile of v1, /device:TPU:114, one launch (start us, length us, event | category | flops | bytes accessed | tf_op | source)
XLA Modules:
  0.0 358.7 jit_solution(2414786802877356116)
XLA Ops:
  8.0 2.4 fusion.14
  17.3 2.2 copy-done.13
  19.5 46.9 %child_factor.1.t_ref = f32[1024,1024]{1,0:T(8,128)S(1)} custom-call(f32[1024,1024]{1,0:T(8,128)S(1)} %bitcast.50), custom_call_target="tpu_custom_call" | custom-call | flops 40000000000 | bytes 12582912 | tf_op jit(solution)/shard_map/child_factor/pallas_call | solution.py:180
  66.8 4.4 %child_rows.1 = (bf16[1024,1024]{1,0:T(8,128)(2,1)S(1)}, bf16[1024,1024]{1,0:T(8,128)(2,1)S(1)}, f32[256,1024]{1,0:T(8,128)}) custom-call(f32[1024,1024]{1,0:T(8,128)S(1)} %child_factor.1.t_ref, f32[256,1024]{1,0:T(8,128)S(1)} %bitcast.47), custom_call_target="tpu_custom_call" | custom-call | flops 2000000000 | bytes 10485760 | tf_op jit(solution)/shard_map/child_rows/pallas_call | solution.py:250
  74.0 49.4 %all-gather.5.cloned.1.call-done = f32[1,4096,1024]{2,1,0:T(8,128)} async-done(((f32[1,256,1024]{2,1,0:T(8,128)}), f32[1,4096,1024]{2,1,0:T(8,128)}) %all-gather.5.cloned.1.call-update) | async-done | bytes 16777232 | tf_op jit(solution)/shard_map/all_gather | solution.py:548
  126.5 9.5 %shard_map.60 = (bf16[1024,512]{1,0:T(8,128)(2,1)S(1)}, bf16[1024,512]{1,0:T(8,128)(2,1)S(1)}) custom-call(s32[4]{0:T(128)S(1)} %slice.76.where_ref, s32[4]{0:T(128)S(1)} %slice.77.there_ref, bf16[1024,1024]{1,0:T(8,128)(2,1)S(1)} %copy-done.4, bf16[1024,1024]{1,0:T(8,128)(2,1)S(1)} %copy-done.7, f32[4096,1024]{1,0:T(8,128)} %bitcast.52), custom_call_target="tpu_custom_call" | custom-call | flops 3000000000 | bytes 8388608 | tf_op jit(solution)/shard_map/pallas_call | solution.py:316
  136.0 6.7 %shard_map.61 = (f32[4,128,512]{2,1,0:T(8,128)S(1)}, f32[4,128,512]{2,1,0:T(8,128)S(1)}) custom-call(s32[8]{0:T(128)S(1)} %slice.73.where_ref, s32[8]{0:T(128)S(1)} %slice.74.there_ref, s32[8]{0:T(128)S(1)} %slice.75.spot_ref, s32[6]{0:T(128)S(1)} %stack.87.place_ref, bf16[1024,512]{1,0:T(8,128)(2,1)S(1)} %get-tuple-element.45.high_ref, ...), custom_call_target="tpu_custom_call" | custom-call | flops 3000000000 | bytes 8388608 | tf_op jit(solution)/shard_map/pallas_call | solution.py:316
  142.9 2.6 collective-permute-done.19
  149.4 5.6 %collective-permute-done.20 = f32[128,512]{1,0:T(8,128)S(1)} collective-permute-done((f32[128,512]{1,0:T(8,128)S(1)}, f32[128,512]{1,0:T(8,128)S(1)}, u32[]{:S(2)}, u32[]{:S(2)}) %collective-permute-start.20) | collective-permute-done | bytes 262176 | tf_op jit(solution)/shard_map/ppermute | solution.py:508
  156.6 4.5 %collective-permute-done.21 = f32[128,512]{1,0:T(8,128)S(1)} collective-permute-done((f32[128,512]{1,0:T(8,128)S(1)}, f32[128,512]{1,0:T(8,128)S(1)}, u32[]{:S(2)}, u32[]{:S(2)}) %collective-permute-start.21) | collective-permute-done | bytes 262176 | tf_op jit(solution)/shard_map/ppermute | solution.py:508
  162.0 23.2 %schur.1 = f32[8192,512]{1,0:T(8,128)} custom-call(s32[32]{0:T(128)} %copy-done.23, s32[32]{0:T(128)} %select_reduce_fusion.absent_ref, f32[4096,1024]{1,0:T(8,128)} %bitcast.54, bf16[1024,512]{1,0:T(8,128)(2,1)} %copy-done.11, bf16[1024,512]{1,0:T(8,128)(2,1)} %copy-done.12), custom_call_target="tpu_custom_call" | custom-call | flops 12884901888 | bytes 37748736 | tf_op jit(solution)/shard_map/schur/pallas_call | solution.py:474
  188.4 7.0 %shard_map.59 = (f32[256,128]{1,0:T(8,128)S(1)}, f32[256,128]{1,0:T(8,128)S(1)}) custom-call(s32[5]{0:T(128)S(1)} %bitcast.49, s32[5]{0:T(128)S(1)} %bitcast.48, s32[6]{0:T(128)S(1)} %stack.87.place_ref, bf16[1024,1024]{1,0:T(8,128)(2,1)S(1)} %copy-done.5, bf16[1024,1024]{1,0:T(8,128)(2,1)S(1)} %copy-done.8, f32[512,128]{1,0:T(8,128)S(1)} %add_add_fusion.own_ref, ...), custom_call_target="tpu_custom_call" | custom-call | flops 3000000000 | bytes 8388608 | tf_op jit(solution)/shard_map/pallas_call | solution.py:316
  197.0 2.6 collective-permute-start.10
  201.5 6.7 %collective-permute-done.11 = f32[256,128]{1,0:T(8,128)S(1)} collective-permute-done((f32[256,128]{1,0:T(8,128)S(1)}, f32[256,128]{1,0:T(8,128)S(1)}, u32[]{:S(2)}, u32[]{:S(2)}) %collective-permute-start.11) | collective-permute-done | bytes 131104 | tf_op jit(solution)/shard_map/ppermute | solution.py:508
  210.7 2.9 collective-permute-start.13
  215.6 2.3 collective-permute-start.17
  219.5 4.2 %collective-permute-start.29 = (f32[128,512]{1,0:T(8,128)S(1)}, f32[128,512]{1,0:T(8,128)}, u32[]{:S(2)}, u32[]{:S(2)}) collective-permute-start(f32[128,512]{1,0:T(8,128)S(1)} %copy-done.17), channel_id=1, source_target_pairs={{0,0},{1,1},{2,16},{3,17},{4,32},{5,33},{6,48},{7,49},{8,64},{9,65... | collective-permute-start | bytes 786440 | tf_op jit(solution)/shard_map/ppermute | solution.py:627
  224.6 2.5 collective-permute-start.25
  227.2 10.9 %collective-permute-done.29 = f32[128,512]{1,0:T(8,128)} collective-permute-done((f32[128,512]{1,0:T(8,128)S(1)}, f32[128,512]{1,0:T(8,128)}, u32[]{:S(2)}, u32[]{:S(2)}) %collective-permute-start.29) | collective-permute-done | bytes 262176 | tf_op jit(solution)/shard_map/ppermute | solution.py:627
  239.1 2.3 collective-permute-start.37
  241.4 3.3 collective-permute-start.36
  247.9 2.5 collective-permute-start.32
  250.4 4.8 %collective-permute-start.24 = (f32[4,256,128]{2,1,0:T(8,128)S(1)}, f32[4,256,128]{2,1,0:T(8,128)}, u32[]{:S(2)}, u32[]{:S(2)}) collective-permute-start(f32[4,256,128]{2,1,0:T(8,128)S(1)} %pad_maximum_fusion.refs_0_), channel_id=1, source_target_pairs={{0,8},{1,9},{2,10},{3,11},{4,12},{5,13},{6,14},{7,15},{8,0},{9,1},... | collective-permute-start | bytes 1572872 | tf_op jit(solution)/shard_map/ppermute | solution.py:512
  256.6 3.5 collective-permute-start.27
  266.9 4.1 %collective-permute-start.35 = (f32[4,64,512]{2,1,0:T(8,128)S(1)}, f32[4,64,512]{2,1,0:T(8,128)S(1)}, u32[]{:S(2)}, u32[]{:S(2)}) collective-permute-start(f32[4,64,512]{2,1,0:T(8,128)S(1)} %pad_maximum_fusion.2.refs_0_), channel_id=1, source_target_pairs={{0,12},{1,13},{2,14},{3,15},{4,0},{5,1},{6,2},{7,3},{8,4},{9,5},{1... | collective-permute-start | bytes 1572872 | tf_op jit(solution)/shard_map/ppermute | solution.py:512
  270.9 7.8 %collective-permute-done.23.refs_1_ = f32[4,256,128]{2,1,0:T(8,128)} collective-permute-done((f32[4,256,128]{2,1,0:T(8,128)S(1)}, f32[4,256,128]{2,1,0:T(8,128)}, u32[]{:S(2)}, u32[]{:S(2)}) %collective-permute-start.23) | collective-permute-done | bytes 524320 | tf_op jit(solution)/shard_map/ppermute | solution.py:512
  280.5 2.2 collective-permute-start.33
  283.8 2.9 collective-permute-start.40
  286.7 26.3 %shard_map.62 = (f32[1024,1024]{1,0:T(8,128)S(1)}, f32[1024,512]{1,0:T(8,128)S(1)}) custom-call(s32[6]{0:T(128)S(1)} %stack.87.place_ref, f32[4,256,128]{2,1,0:T(8,128)S(1)} %pad_maximum_fusion.refs_0_, f32[4,256,128]{2,1,0:T(8,128)} %collective-permute-done.23.refs_1_, f32[4,256,128]{2,1,0:T(8,128)} %collective-permute-done.24.refs_2_, ...), custom_call_target="tpu_custom_call" | custom-call | flops 10000000000 | bytes 12582912 | tf_op jit(solution)/shard_map/pallas_call | solution.py:207
  314.8 21.0 %shard_map.63 = (f32[1024,1024]{1,0:T(8,128)S(1)}, f32[1024,512]{1,0:T(8,128)S(1)}) custom-call(f32[1024,1024]{1,0:T(8,128)S(1)} %get-tuple-element.52.t_in), custom_call_target="tpu_custom_call" | custom-call | flops 10000000000 | bytes 12582912 | tf_op jit(solution)/shard_map/pallas_call | solution.py:212
  335.8 10.7 %solve.1 = f32[1024,512]{1,0:T(8,128)S(1)} custom-call(s32[6]{0:T(128)S(1)} %stack.87.place_ref, f32[1024,1024]{1,0:T(8,128)S(1)} %get-tuple-element.53.t_ref, f32[1024,512]{1,0:T(8,128)S(1)} %get-tuple-element.54.first_ref, f32[1024,512]{1,0:T(8,128)S(1)} %get-tuple-element.55.second_ref, f32[8,128,512]{2,1,0:T(8,128)S(1)} %bitcast.51, ...), custom_call_target="tpu_custom_call" | custom-call | flops 10000000000 | bytes 20971520 | tf_op jit(solution)/shard_map/solve/pallas_call | solution.py:410
  347.9 4.1 %select_subtract_fusion = f32[1024,512]{1,0:T(8,128)} fusion(f32[1024,512]{1,0:T(8,128)} %copy-done.9, f32[1024,512]{1,0:T(8,128)S(1)} %copy-done.2, f32[1024,512]{1,0:T(8,128)} %reduce-scatter.2.cloned.1.call-done, pred[1024]{0:T(1024)(128)(4,1)S(1)} %fusion.7), kind=kLoop, calls=%fused_computation | loop fusion | flops 1572864 | bytes 8389632 | tf_op jit(solution)/shard_map/sub | solution.py:646
  (146 shorter events, 52.1 us)
Async XLA Ops:
  7.2 116.2 %all-gather.5.cloned.1.call-start = ((), (), s32[]{:S(2)}) async-start(), calls=%async_computation.2 | async-start | bytes 17825792 | tf_op jit(solution)/shard_map/all_gather | solution.py:548
  7.9 216.7 %all-gather.7.cloned.1.call-start = ((), (), s32[]{:S(2)}) async-start(), calls=%async_computation.3 | async-start | bytes 2359296 | tf_op jit(solution)/shard_map/all_gather | solution.py:628
  12.4 61.5 %collective-permute-start.5 = (f32[512,128]{1,0:T(8,128)}, f32[512,128]{1,0:T(8,128)S(1)}, u32[]{:S(2)}, u32[]{:S(2)}) collective-permute-start(f32[512,128]{1,0:T(8,128)} %get-tuple-element.63), channel_id=1, source_target_pairs={{0,5},{1,13}} | collective-permute-start | bytes 786440 | tf_op jit(solution)/shard_map/ppermute | solution.py:554
  13.1 60.8 %collective-permute-start.4 = (f32[512,128]{1,0:T(8,128)S(1)}, f32[512,128]{1,0:T(8,128)S(1)}, u32[]{:S(2)}, u32[]{:S(2)}) collective-permute-start(f32[512,128]{1,0:T(8,128)S(1)} %get-tuple-element.64), channel_id=1, source_target_pairs={{0,4},{1,12}} | collective-permute-start | bytes 786440 | tf_op jit(solution)/shard_map/ppermute | solution.py:554
  15.1 58.8 %collective-permute-start.3 = (f32[512,128]{1,0:T(8,128)S(1)}, f32[512,128]{1,0:T(8,128)S(1)}, u32[]{:S(2)}, u32[]{:S(2)}) collective-permute-start(f32[512,128]{1,0:T(8,128)S(1)} %get-tuple-element.65), channel_id=1, source_target_pairs={{0,3},{1,11}} | collective-permute-start | bytes 786440 | tf_op jit(solution)/shard_map/ppermute | solution.py:554
  15.8 58.1 %collective-permute-start.2 = (f32[512,128]{1,0:T(8,128)S(1)}, f32[512,128]{1,0:T(8,128)S(1)}, u32[]{:S(2)}, u32[]{:S(2)}) collective-permute-start(f32[512,128]{1,0:T(8,128)S(1)} %get-tuple-element.66), channel_id=1, source_target_pairs={{0,2},{1,10}} | collective-permute-start | bytes 786440 | tf_op jit(solution)/shard_map/ppermute | solution.py:554
  16.5 57.4 %collective-permute-start = (f32[512,128]{1,0:T(8,128)S(1)}, f32[512,128]{1,0:T(8,128)S(1)}, u32[]{:S(2)}, u32[]{:S(2)}) collective-permute-start(f32[512,128]{1,0:T(8,128)S(1)} %get-tuple-element.67), channel_id=1, source_target_pairs={{0,0},{1,8}} | collective-permute-start | bytes 786440 | tf_op jit(solution)/shard_map/ppermute | solution.py:554
  145.8 9.2 %collective-permute-start.20 = (f32[128,512]{1,0:T(8,128)S(1)}, f32[128,512]{1,0:T(8,128)S(1)}, u32[]{:S(2)}, u32[]{:S(2)}) collective-permute-start(f32[128,512]{1,0:T(8,128)S(1)} %get-tuple-element.68), channel_id=1, source_target_pairs={{0,32},{16,48},{32,64},{48,80},{64,96},{80,112},{96,0},{112,16},{1... | collective-permute-start | bytes 786440 | tf_op jit(solution)/shard_map/ppermute | solution.py:508
  145.9 10.8 %collective-permute-start.22 = (f32[128,512]{1,0:T(8,128)S(1)}, f32[128,512]{1,0:T(8,128)S(1)}, u32[]{:S(2)}, u32[]{:S(2)}) collective-permute-start(f32[128,512]{1,0:T(8,128)S(1)} %get-tuple-element.69), channel_id=1, source_target_pairs={{0,96},{16,112},{32,0},{48,16},{64,32},{80,48},{96,64},{112,80},{1... | collective-permute-start | bytes 786440 | tf_op jit(solution)/shard_map/ppermute | solution.py:508
  147.9 13.2 %collective-permute-start.21 = (f32[128,512]{1,0:T(8,128)S(1)}, f32[128,512]{1,0:T(8,128)S(1)}, u32[]{:S(2)}, u32[]{:S(2)}) collective-permute-start(f32[128,512]{1,0:T(8,128)S(1)} %get-tuple-element.70), channel_id=1, source_target_pairs={{0,64},{16,80},{32,96},{48,112},{64,0},{80,16},{96,32},{112,48},{1... | collective-permute-start | bytes 786440 | tf_op jit(solution)/shard_map/ppermute | solution.py:508
  161.9 186.0 %reduce-scatter.2.cloned.1.call-start = ((), (), s32[]{:S(2)}) async-start(), calls=%async_computation.1 | async-start | bytes 18874368 | tf_op jit(solution)/shard_map/reduce_scatter | solution.py:631
  196.9 11.2 %collective-permute-start.11 = (f32[256,128]{1,0:T(8,128)S(1)}, f32[256,128]{1,0:T(8,128)S(1)}, u32[]{:S(2)}, u32[]{:S(2)}) collective-permute-start(f32[256,128]{1,0:T(8,128)S(1)} %add.169), channel_id=1, source_target_pairs={{0,96},{16,112},{32,0},{48,16},{64,32},{80,48},{96,64},{112,80},{1... | collective-permute-start | bytes 393224 | tf_op jit(solution)/shard_map/ppermute | solution.py:508
  197.0 11.5 %collective-permute-start.10 = (f32[256,128]{1,0:T(8,128)S(1)}, f32[256,128]{1,0:T(8,128)S(1)}, u32[]{:S(2)}, u32[]{:S(2)}) collective-permute-start(f32[256,128]{1,0:T(8,128)S(1)} %add.169), channel_id=1, source_target_pairs={{0,64},{16,80},{32,96},{48,112},{64,0},{80,16},{96,32},{112,48},{1... | collective-permute-start | bytes 393224 | tf_op jit(solution)/shard_map/ppermute | solution.py:508
  199.6 10.9 %collective-permute-start.9 = (f32[256,128]{1,0:T(8,128)S(1)}, f32[256,128]{1,0:T(8,128)S(1)}, u32[]{:S(2)}, u32[]{:S(2)}) collective-permute-start(f32[256,128]{1,0:T(8,128)S(1)} %add.169), channel_id=1, source_target_pairs={{0,32},{16,48},{32,64},{48,80},{64,96},{80,112},{96,0},{112,16},{1... | collective-permute-start | bytes 393224 | tf_op jit(solution)/shard_map/ppermute | solution.py:508
  210.7 8.8 %collective-permute-start.13 = (f32[256,128]{1,0:T(8,128)S(1)}, f32[256,128]{1,0:T(8,128)S(1)}, u32[]{:S(2)}, u32[]{:S(2)}) collective-permute-start(f32[256,128]{1,0:T(8,128)S(1)} %add_add_fusion.1), channel_id=1, source_target_pairs={{0,2},{1,3},{2,0},{3,1},{4,6},{5,7},{6,4},{7,5},{8,10},{9,11},{10,... | collective-permute-start | bytes 393224 | tf_op jit(solution)/shard_map/ppermute | solution.py:516
  213.6 10.1 %collective-permute-start.12 = (f32[256,128]{1,0:T(8,128)S(1)}, f32[256,128]{1,0:T(8,128)S(1)}, u32[]{:S(2)}, u32[]{:S(2)}) collective-permute-start(f32[256,128]{1,0:T(8,128)S(1)} %add_add_fusion.1), channel_id=1, source_target_pairs={{0,1},{1,2},{2,3},{3,0},{4,5},{5,6},{6,7},{7,4},{8,9},{9,10},{10,1... | collective-permute-start | bytes 393224 | tf_op jit(solution)/shard_map/ppermute | solution.py:516
  215.0 8.8 %collective-permute-start.18 = (f32[256,128]{1,0:T(8,128)S(1)}, f32[256,128]{1,0:T(8,128)S(1)}, u32[]{:S(2)}, u32[]{:S(2)}) collective-permute-start(f32[256,128]{1,0:T(8,128)S(1)} %collective-permute-done.15), channel_id=1, source_target_pairs={{0,12},{1,13},{2,14},{3,15},{4,0},{5,1},{6,2},{7,3},{8,4},{9,5},{1... | collective-permute-start | bytes 393224 | tf_op jit(solution)/shard_map/ppermute | solution.py:512
  219.5 18.6 %collective-permute-start.29 = (f32[128,512]{1,0:T(8,128)S(1)}, f32[128,512]{1,0:T(8,128)}, u32[]{:S(2)}, u32[]{:S(2)}) collective-permute-start(f32[128,512]{1,0:T(8,128)S(1)} %copy-done.17), channel_id=1, source_target_pairs={{0,0},{1,1},{2,16},{3,17},{4,32},{5,33},{6,48},{7,49},{8,64},{9,65... | collective-permute-start | bytes 786440 | tf_op jit(solution)/shard_map/ppermute | solution.py:627
  224.6 35.5 %collective-permute-start.25 = (f32[4,256,128]{2,1,0:T(8,128)S(1)}, f32[4,256,128]{2,1,0:T(8,128)S(1)}, u32[]{:S(2)}, u32[]{:S(2)}) collective-permute-start(f32[4,256,128]{2,1,0:T(8,128)S(1)} %pad_maximum_fusion.refs_0_), channel_id=1, source_target_pairs={{0,12},{1,13},{2,14},{3,15},{4,0},{5,1},{6,2},{7,3},{8,4},{9,5},{1... | collective-permute-start | bytes 1572872 | tf_op jit(solution)/shard_map/ppermute | solution.py:512
  244.6 10.6 %collective-permute-start.31 = (f32[64,512]{1,0:T(8,128)S(1)}, f32[64,512]{1,0:T(8,128)S(1)}, u32[]{:S(2)}, u32[]{:S(2)}) collective-permute-start(f32[64,512]{1,0:T(8,128)S(1)} %get-tuple-element.74), channel_id=1, source_target_pairs={{0,2},{1,3},{2,0},{3,1},{4,6},{5,7},{6,4},{7,5},{8,10},{9,11},{10,... | collective-permute-start | bytes 393224 | tf_op jit(solution)/shard_map/ppermute | solution.py:516
  246.8 9.1 %collective-permute-start.30 = (f32[64,512]{1,0:T(8,128)S(1)}, f32[64,512]{1,0:T(8,128)S(1)}, u32[]{:S(2)}, u32[]{:S(2)}) collective-permute-start(f32[64,512]{1,0:T(8,128)S(1)} %get-tuple-element.74), channel_id=1, source_target_pairs={{0,1},{1,2},{2,3},{3,0},{4,5},{5,6},{6,7},{7,4},{8,9},{9,10},{10,1... | collective-permute-start | bytes 393224 | tf_op jit(solution)/shard_map/ppermute | solution.py:516
  250.4 16.5 %collective-permute-start.24 = (f32[4,256,128]{2,1,0:T(8,128)S(1)}, f32[4,256,128]{2,1,0:T(8,128)}, u32[]{:S(2)}, u32[]{:S(2)}) collective-permute-start(f32[4,256,128]{2,1,0:T(8,128)S(1)} %pad_maximum_fusion.refs_0_), channel_id=1, source_target_pairs={{0,8},{1,9},{2,10},{3,11},{4,12},{5,13},{6,14},{7,15},{8,0},{9,1},... | collective-permute-start | bytes 1572872 | tf_op jit(solution)/shard_map/ppermute | solution.py:512
  255.2 23.6 %collective-permute-start.23 = (f32[4,256,128]{2,1,0:T(8,128)S(1)}, f32[4,256,128]{2,1,0:T(8,128)}, u32[]{:S(2)}, u32[]{:S(2)}) collective-permute-start(f32[4,256,128]{2,1,0:T(8,128)S(1)} %pad_maximum_fusion.refs_0_), channel_id=1, source_target_pairs={{0,4},{1,5},{2,6},{3,7},{4,8},{5,9},{6,10},{7,11},{8,12},{9,13},{1... | collective-permute-start | bytes 1572872 | tf_op jit(solution)/shard_map/ppermute | solution.py:512
  256.0 24.5 %collective-permute-start.28 = (f32[4,256,128]{2,1,0:T(8,128)S(1)}, f32[4,256,128]{2,1,0:T(8,128)}, u32[]{:S(2)}, u32[]{:S(2)}) collective-permute-start(f32[4,256,128]{2,1,0:T(8,128)S(1)} %pad_maximum_fusion.1.refs_4_), channel_id=1, source_target_pairs={{0,3},{1,0},{2,1},{3,2},{4,7},{5,4},{6,5},{7,6},{8,11},{9,8},{10,9... | collective-permute-start | bytes 1572872 | tf_op jit(solution)/shard_map/ppermute | solution.py:516
  256.6 26.1 %collective-permute-start.27 = (f32[4,256,128]{2,1,0:T(8,128)S(1)}, f32[4,256,128]{2,1,0:T(8,128)}, u32[]{:S(2)}, u32[]{:S(2)}) collective-permute-start(f32[4,256,128]{2,1,0:T(8,128)S(1)} %pad_maximum_fusion.1.refs_4_), channel_id=1, source_target_pairs={{0,2},{1,3},{2,0},{3,1},{4,6},{5,7},{6,4},{7,5},{8,10},{9,11},{10,... | collective-permute-start | bytes 1572872 | tf_op jit(solution)/shard_map/ppermute | solution.py:516
  260.9 22.9 %collective-permute-start.26 = (f32[4,256,128]{2,1,0:T(8,128)S(1)}, f32[4,256,128]{2,1,0:T(8,128)}, u32[]{:S(2)}, u32[]{:S(2)}) collective-permute-start(f32[4,256,128]{2,1,0:T(8,128)S(1)} %pad_maximum_fusion.1.refs_4_), channel_id=1, source_target_pairs={{0,1},{1,2},{2,3},{3,0},{4,5},{5,6},{6,7},{7,4},{8,9},{9,10},{10,1... | collective-permute-start | bytes 1572872 | tf_op jit(solution)/shard_map/ppermute | solution.py:516
  266.9 46.2 %collective-permute-start.35 = (f32[4,64,512]{2,1,0:T(8,128)S(1)}, f32[4,64,512]{2,1,0:T(8,128)S(1)}, u32[]{:S(2)}, u32[]{:S(2)}) collective-permute-start(f32[4,64,512]{2,1,0:T(8,128)S(1)} %pad_maximum_fusion.2.refs_0_), channel_id=1, source_target_pairs={{0,12},{1,13},{2,14},{3,15},{4,0},{5,1},{6,2},{7,3},{8,4},{9,5},{1... | collective-permute-start | bytes 1572872 | tf_op jit(solution)/shard_map/ppermute | solution.py:512
  278.8 57.0 %collective-permute-start.34 = (f32[4,64,512]{2,1,0:T(8,128)S(1)}, f32[4,64,512]{2,1,0:T(8,128)S(1)}, u32[]{:S(2)}, u32[]{:S(2)}) collective-permute-start(f32[4,64,512]{2,1,0:T(8,128)S(1)} %pad_maximum_fusion.2.refs_0_), channel_id=1, source_target_pairs={{0,8},{1,9},{2,10},{3,11},{4,12},{5,13},{6,14},{7,15},{8,0},{9,1},... | collective-permute-start | bytes 1572872 | tf_op jit(solution)/shard_map/ppermute | solution.py:512
  280.5 55.3 %collective-permute-start.33 = (f32[4,64,512]{2,1,0:T(8,128)S(1)}, f32[4,64,512]{2,1,0:T(8,128)S(1)}, u32[]{:S(2)}, u32[]{:S(2)}) collective-permute-start(f32[4,64,512]{2,1,0:T(8,128)S(1)} %pad_maximum_fusion.2.refs_0_), channel_id=1, source_target_pairs={{0,4},{1,5},{2,6},{3,7},{4,8},{5,9},{6,10},{7,11},{8,12},{9,13},{1... | collective-permute-start | bytes 1572872 | tf_op jit(solution)/shard_map/ppermute | solution.py:512
  282.7 53.1 %collective-permute-start.41 = (f32[4,64,512]{2,1,0:T(8,128)S(1)}, f32[4,64,512]{2,1,0:T(8,128)S(1)}, u32[]{:S(2)}, u32[]{:S(2)}) collective-permute-start(f32[4,64,512]{2,1,0:T(8,128)S(1)} %pad_maximum_fusion.3.refs_4_), channel_id=1, source_target_pairs={{0,3},{1,0},{2,1},{3,2},{4,7},{5,4},{6,5},{7,6},{8,11},{9,8},{10,9... | collective-permute-start | bytes 1572872 | tf_op jit(solution)/shard_map/ppermute | solution.py:516
  283.8 52.0 %collective-permute-start.40 = (f32[4,64,512]{2,1,0:T(8,128)S(1)}, f32[4,64,512]{2,1,0:T(8,128)S(1)}, u32[]{:S(2)}, u32[]{:S(2)}) collective-permute-start(f32[4,64,512]{2,1,0:T(8,128)S(1)} %pad_maximum_fusion.3.refs_4_), channel_id=1, source_target_pairs={{0,2},{1,3},{2,0},{3,1},{4,6},{5,7},{6,4},{7,5},{8,10},{9,11},{10,... | collective-permute-start | bytes 1572872 | tf_op jit(solution)/shard_map/ppermute | solution.py:516
  313.0 22.8 %collective-permute-start.39 = (f32[4,64,512]{2,1,0:T(8,128)S(1)}, f32[4,64,512]{2,1,0:T(8,128)S(1)}, u32[]{:S(2)}, u32[]{:S(2)}) collective-permute-start(f32[4,64,512]{2,1,0:T(8,128)S(1)} %pad_maximum_fusion.3.refs_4_), channel_id=1, source_target_pairs={{0,1},{1,2},{2,3},{3,0},{4,5},{5,6},{6,7},{7,4},{8,9},{9,10},{10,1... | collective-permute-start | bytes 1572872 | tf_op jit(solution)/shard_map/ppermute | solution.py:516
  (37 other events, 334.2 us)
Sparse Core Ops, SparseCore 0:
  10.1 113.1 all-gather.4
  162.1 24.6 all-gather.6
  189.2 98.7 reduce-scatter.1
